TPU v7x, 32 devices: a whole 2x2x4 slice. The times are simulated.
32 devices in a mesh: section: 4 (over y, x), expert: 8 (over z, core).
Axes of the slice: x: 2, y: 2, z: 4, core: 2. Of those that a mesh axis runs over, the one named last changes fastest.
Arguments:
- tokens: bfloat16 [2, 256, 7168], P(None, 'expert'), may hold values from -6 to 6
- norm_gain: float32 [4, 7168], P('section'), may hold values from 0.25 to 1.75
- w_gate: bfloat16 [4, 7168, 2048], P('section', None, 'expert'), may hold values from -0.0625 to 0.0625
- w_up: bfloat16 [4, 7168, 2048], P('section', None, 'expert'), may hold values from -0.0625 to 0.0625
- w_down: bfloat16 [4, 2048, 7168], P('section', 'expert'), may hold values from -0.1875 to 0.1875
- expert_ids: int32 [4, 2, 256, 1], P('section', None, 'expert'), may hold values from 0 to 1; in each aligned block of 32 rows (0 to 31, 32 to 63, ..., all dimensions but the last counted through in order) at most 24 rows name the same one
- gate_weight: float32 [4, 2, 256, 1], P('section', None, 'expert'), may hold values from 0.3 to 1.5
- capacity: int32 [4, 2], P('section'), may hold values from 64 to 192
Outputs:
- results: bfloat16 [2, 256, 7168], P(None, 'expert', 'section')
Inputs may be any that keep to these rules, and one draw needn't show every extreme that they name: `expert_ids`: A token's 1 expert differ. In each aligned block of 32 tokens (the tokens of one device in one span and layer) no expert is named by more than 24 tokens, a bound that some block reaches.
All inputs are finite; a program needn't handle non-finite values.
Results may differ from a plain program's by a relative error of at most 0.0095.
Values may be sent and summed in bfloat16 or wider, within the bound.
No kernel may reach another device: no remote copies, remote signals or barrier semaphores. Data moves between devices by JAX's collectives and lax.ppermute only.
A program may use at most 128 MiB of HBM per device.

v0:
```python
import jax
import jax.numpy as jnp
from jax import lax
from jax.sharding import PartitionSpec as P

EPSILON = 1e-06


def entering(array, axis, combine, identity):
    length, place = (lax.axis_size(axis), lax.axis_index(axis))
    everything = lax.all_gather(array, axis)
    start = jnp.broadcast_to(jnp.asarray(identity, array.dtype), array.shape)

    def hop(k, before):
        reached = k < place
        new = combine(before, everything[k])
        return jnp.where(reached, new, before)

    return lax.fori_loop(0, length, hop, start)


def shifted(array, axis, by):
    length = lax.axis_size(axis)
    pairs = [(i, i + by) for i in range(length) if 0 <= i + by < length]
    return lax.ppermute(array, axis, pairs)


def slot_numbers(routed):
    length = routed.shape[-1]
    order = jnp.arange(length, dtype=jnp.int32)
    earlier = order[:, None] > order[None, :]
    alike = routed[..., :, None] == routed[..., None, :]
    return jnp.sum((alike & earlier).astype(jnp.int32), axis=-1)


def add_counts(earlier_counts, later_counts):
    return earlier_counts + later_counts


def expert_rows(arrived, gate_cols, up_cols, down_rows):
    width = arrived.shape[-1]
    flat_rows = arrived.reshape(-1, width)
    gate_out = jnp.dot(flat_rows, gate_cols, preferred_element_type=jnp.float32)
    up_out = jnp.dot(flat_rows, up_cols, preferred_element_type=jnp.float32)
    hidden = (jax.nn.silu(gate_out) * up_out).astype(jnp.bfloat16)
    partial_out = jnp.dot(hidden, down_rows, preferred_element_type=jnp.float32).astype(
        jnp.bfloat16
    )
    return partial_out.reshape(arrived.shape)


def moe_layer(
    stream, gain, gate_cols, up_cols, down_rows, routed_ids, gate_values, limits, slot_count
):
    token_rows, width = stream.shape
    top_count = routed_ids.shape[-1]
    expert_total = limits.shape[0]
    device_count = lax.axis_size("expert")
    split_count = device_count // expert_total
    widened = stream.astype(jnp.float32)
    stats = jnp.mean(widened * widened, axis=-1, keepdims=True)
    normed = (widened * lax.rsqrt(stats + EPSILON) * gain[None, :]).astype(jnp.bfloat16)
    flat_ids = routed_ids.reshape(-1)
    slots = slot_numbers(flat_ids)
    expert_iota = jnp.arange(expert_total, dtype=jnp.int32)
    onehot_ids = (flat_ids[:, None] == expert_iota[None, :]).astype(jnp.int32)
    counts = jnp.sum(onehot_ids, axis=0)
    before = entering(counts, "expert", add_counts, jnp.zeros_like(counts))
    queue = jnp.sum(onehot_ids * before[None, :], axis=1) + slots
    bound = jnp.sum(onehot_ids * limits[None, :], axis=1)
    weights = jnp.where(queue < bound, gate_values.reshape(-1), jnp.float32(0.0))
    target = flat_ids * slot_count + slots
    buffer_iota = jnp.arange(expert_total * slot_count, dtype=jnp.int32)
    placed = (buffer_iota[None, :] == target[:, None]).astype(jnp.float32)
    select = jnp.sum(placed.reshape(token_rows, top_count, -1), axis=1).astype(jnp.bfloat16)
    packed = lax.dot_general(
        select, normed, (((0,), (0,)), ((), ())), preferred_element_type=jnp.float32
    ).astype(jnp.bfloat16)
    outgoing = jnp.repeat(packed.reshape(expert_total, slot_count, width), split_count, axis=0)
    partials = expert_rows(
        lax.all_to_all(outgoing, "expert", split_axis=0, concat_axis=0, tiled=True),
        gate_cols,
        up_cols,
        down_rows,
    )
    returned = lax.all_to_all(partials, "expert", split_axis=0, concat_axis=0, tiled=True)
    summed = jnp.sum(
        returned.reshape(expert_total, split_count, slot_count, width).astype(jnp.float32), axis=1
    ).reshape(-1, width)
    mixing = jnp.sum((placed * weights[:, None]).reshape(token_rows, top_count, -1), axis=1)
    moe_out = jnp.dot(
        mixing, summed, precision=lax.Precision.HIGHEST, preferred_element_type=jnp.float32
    )
    return (widened + moe_out).astype(jnp.bfloat16)


def body(tokens, norm_gain, w_gate, w_up, w_down, expert_ids, gate_weight, capacity):
    section_count = lax.axis_size("section")
    section_index = lax.axis_index("section")
    span_count, token_rows, width = tokens.shape
    top_count = expert_ids.shape[-1]
    expert_total = capacity.shape[-1]
    slot_count = min(token_rows, max(2, 3 * (token_rows * top_count) // (2 * expert_total)))
    held = jnp.zeros((token_rows, width), jnp.bfloat16)
    results = jnp.zeros((span_count, token_rows, width), jnp.bfloat16)
    moments = section_count + span_count - 1
    for moment in range(moments):
        position = moment - section_index
        active = (position >= 0) & (position < span_count)
        picked = jnp.clip(position, 0, span_count - 1)
        entry = tokens[min(moment, span_count - 1)]
        stream = jnp.where(section_index == 0, entry, held)
        routed = lax.dynamic_index_in_dim(expert_ids[0], picked, 0, keepdims=False)
        gates = lax.dynamic_index_in_dim(gate_weight[0], picked, 0, keepdims=False)
        layer_out = moe_layer(
            stream,
            norm_gain[0],
            w_gate[0],
            w_up[0],
            w_down[0],
            routed,
            gates,
            capacity[0],
            slot_count,
        )
        finished = active & (section_index == section_count - 1)
        results = jnp.where(
            finished, lax.dynamic_update_index_in_dim(results, layer_out, picked, 0), results
        )
        if moment + 1 < moments:
            held = shifted(layer_out, "section", 1)
    collected = lax.psum_scatter(
        results.astype(jnp.float32).astype(jnp.bfloat16), "section", scatter_dimension=2, tiled=True
    )
    return collected


def solution(mesh):
    in_specs = (
        P(None, "expert", None),
        P("section", None),
        P("section", None, "expert"),
        P("section", None, "expert"),
        P("section", "expert", None),
        P("section", None, "expert", None),
        P("section", None, "expert", None),
        P("section", None),
    )
    out_specs = P(None, "expert", "section")
    return jax.shard_map(body, mesh=mesh, in_specs=in_specs, out_specs=out_specs, check_vma=False)
```

profile of v0, /device:TPU:0, one launch (start us, length us, event | category | flops | bytes accessed | tf_op | source)
XLA Modules:
  0.0 837.8 jit_solution(17388975175286004267)
XLA Ops:
  12.2 6.5 all-to-all-start
  21.5 60.4 %all-reduce.5 = (s32[16]{0:T(128)S(1)}, s32[16]{0:T(128)S(1)}, s32[16]{0:T(128)S(1)}, s32[16]{0:T(128)S(1)}, s32[16]{0:T(128)S(1)}) all-reduce(s32[16]{0:T(128)S(1)} %dynamic-update-slice.9, s32[16]{0:T(128)S(1)} %dynamic-update-slice.6, s32[16]{0:T(128)S(1)} %dynamic-update-slice.7, ...), channel_id=6, replica_groups=mesh['section'=4,'expert'=8] {'expert'}, use_global_device_ids=true, to_apply=%add.4 | all-reduce | flops 80 | bytes 640
  82.8 2.9 fusion.31
  85.7 7.8 convolution_convert_fusion.4
  93.5 3.8 all-to-all-start.1
  98.9 61.4 %all-to-all-done.1 = bf16[8,24,7168]{2,1,0:T(8,128)(2,1)S(1)} async-done(((bf16[8,24,7168]{2,1,0:T(8,128)(2,1)}), bf16[8,24,7168]{2,1,0:T(8,128)(2,1)S(1)}, u32[]{:S(2)}, u32[]{:S(2)}) %all-to-all-start.1) | async-done | bytes 2752544 | tf_op jit(solution)/shard_map/all_to_all | solution.py:86
  163.5 3.4 collective-permute-start
  166.9 9.4 %collective-permute-done = bf16[32,7168]{1,0:T(8,128)(2,1)S(1)} collective-permute-done((bf16[32,7168]{1,0:T(8,128)(2,1)S(1)}, bf16[32,7168]{1,0:T(8,128)(2,1)S(1)}, u32[]{:S(2)}, u32[]{:S(2)}) %collective-permute-start) | collective-permute-done | bytes 458784 | tf_op jit(solution)/shard_map/ppermute | solution.py:25
  177.4 66.2 %all_to_all.50 = bf16[8,24,7168]{2,1,0:T(8,128)(2,1)S(1)} all-to-all(bf16[8,24,7168]{2,1,0:T(8,128)(2,1)S(1)} %bitcast.240), channel_id=1, replica_groups=mesh['section'=4,'expert'=8] {'expert'}, dimensions={0} | all-to-all | bytes 5505024 | tf_op jit(solution)/shard_map/all_to_all | solution.py:81
  244.5 7.8 convolution_convert_fusion.3
  252.3 3.6 all-to-all-start.3
  256.1 62.9 %all-to-all-done.3 = bf16[8,24,7168]{2,1,0:T(8,128)(2,1)S(1)} async-done(((bf16[8,24,7168]{2,1,0:T(8,128)(2,1)}), bf16[8,24,7168]{2,1,0:T(8,128)(2,1)S(1)}, u32[]{:S(2)}, u32[]{:S(2)}) %all-to-all-start.3) | async-done | bytes 2752544 | tf_op jit(solution)/shard_map/all_to_all | solution.py:86
  319.3 2.8 fusion.97
  322.1 4.4 collective-permute-start.1
  326.6 9.4 %collective-permute-done.1 = bf16[32,7168]{1,0:T(8,128)(2,1)S(1)} collective-permute-done((bf16[32,7168]{1,0:T(8,128)(2,1)S(1)}, bf16[32,7168]{1,0:T(8,128)(2,1)S(1)}, u32[]{:S(2)}, u32[]{:S(2)}) %collective-permute-start.1) | collective-permute-done | bytes 458784 | tf_op jit(solution)/shard_map/ppermute | solution.py:25
  337.0 66.2 %all_to_all.51 = bf16[8,24,7168]{2,1,0:T(8,128)(2,1)S(1)} all-to-all(bf16[8,24,7168]{2,1,0:T(8,128)(2,1)S(1)} %bitcast.241), channel_id=1, replica_groups=mesh['section'=4,'expert'=8] {'expert'}, dimensions={0} | all-to-all | bytes 5505024 | tf_op jit(solution)/shard_map/all_to_all | solution.py:81
  404.2 7.8 convolution_convert_fusion.2
  412.0 3.6 all-to-all-start.5
  415.8 62.9 %all-to-all-done.5 = bf16[8,24,7168]{2,1,0:T(8,128)(2,1)S(1)} async-done(((bf16[8,24,7168]{2,1,0:T(8,128)(2,1)}), bf16[8,24,7168]{2,1,0:T(8,128)(2,1)S(1)}, u32[]{:S(2)}, u32[]{:S(2)}) %all-to-all-start.5) | async-done | bytes 2752544 | tf_op jit(solution)/shard_map/all_to_all | solution.py:86
  481.8 4.4 collective-permute-start.2
  486.4 9.3 %collective-permute-done.2 = bf16[32,7168]{1,0:T(8,128)(2,1)S(1)} collective-permute-done((bf16[32,7168]{1,0:T(8,128)(2,1)S(1)}, bf16[32,7168]{1,0:T(8,128)(2,1)S(1)}, u32[]{:S(2)}, u32[]{:S(2)}) %collective-permute-start.2) | collective-permute-done | bytes 458784 | tf_op jit(solution)/shard_map/ppermute | solution.py:25
  496.7 66.2 %all_to_all.52 = bf16[8,24,7168]{2,1,0:T(8,128)(2,1)S(1)} all-to-all(bf16[8,24,7168]{2,1,0:T(8,128)(2,1)S(1)} %bitcast.242), channel_id=1, replica_groups=mesh['section'=4,'expert'=8] {'expert'}, dimensions={0} | all-to-all | bytes 5505024 | tf_op jit(solution)/shard_map/all_to_all | solution.py:81
  563.8 7.8 convolution_convert_fusion.1
  571.6 3.6 all-to-all-start.7
  575.4 62.8 %all-to-all-done.7 = bf16[8,24,7168]{2,1,0:T(8,128)(2,1)S(1)} async-done(((bf16[8,24,7168]{2,1,0:T(8,128)(2,1)}), bf16[8,24,7168]{2,1,0:T(8,128)(2,1)S(1)}, u32[]{:S(2)}, u32[]{:S(2)}) %all-to-all-start.7) | async-done | bytes 2752544 | tf_op jit(solution)/shard_map/all_to_all | solution.py:86
  641.4 5.2 collective-permute-start.3
  646.7 9.4 %collective-permute-done.3 = bf16[32,7168]{1,0:T(8,128)(2,1)S(1)} collective-permute-done((bf16[32,7168]{1,0:T(8,128)(2,1)S(1)}, bf16[32,7168]{1,0:T(8,128)(2,1)S(1)}, u32[]{:S(2)}, u32[]{:S(2)}) %collective-permute-start.3) | collective-permute-done | bytes 458784 | tf_op jit(solution)/shard_map/ppermute | solution.py:25
  657.2 66.2 %all_to_all.53 = bf16[8,24,7168]{2,1,0:T(8,128)(2,1)S(1)} all-to-all(bf16[8,24,7168]{2,1,0:T(8,128)(2,1)S(1)} %bitcast.243), channel_id=1, replica_groups=mesh['section'=4,'expert'=8] {'expert'}, dimensions={0} | all-to-all | bytes 5505024 | tf_op jit(solution)/shard_map/all_to_all | solution.py:81
  724.3 7.8 convolution_convert_fusion
  732.1 3.6 all-to-all-start.9
  735.9 62.8 %all-to-all-done.9 = bf16[8,24,7168]{2,1,0:T(8,128)(2,1)S(1)} async-done(((bf16[8,24,7168]{2,1,0:T(8,128)(2,1)}), bf16[8,24,7168]{2,1,0:T(8,128)(2,1)S(1)}, u32[]{:S(2)}, u32[]{:S(2)}) %all-to-all-start.9) | async-done | bytes 2752544 | tf_op jit(solution)/shard_map/all_to_all | solution.py:86
  801.9 29.0 %reduce-scatter.2.cloned.1.call-done = bf16[2,32,1792]{2,1,0:T(8,128)(2,1)} async-done(((bf16[2,32,7168]{2,1,0:T(8,128)(2,1)}), bf16[2,32,1792]{2,1,0:T(8,128)(2,1)}) %reduce-scatter.2.cloned.1.call-update) | async-done | bytes 229392 | tf_op jit(solution)/shard_map/reduce_scatter | solution.py:132
  (147 shorter events, 32.6 us)
Async XLA Ops:
  12.2 6.5 copy-start.11
  12.2 70.6 %all-to-all-start = ((bf16[8,24,7168]{2,1,0:T(8,128)(2,1)}), bf16[8,24,7168]{2,1,0:T(8,128)(2,1)S(1)}, u32[]{:S(2)}, u32[]{:S(2)}) async-start(bf16[8,24,7168]{2,1,0:T(8,128)(2,1)} %bitcast.235), calls=%async_computation | async-start | bytes 5505024 | tf_op jit(solution)/shard_map/all_to_all | solution.py:81
  93.5 5.1 copy-start.10
  93.5 5.2 copy-start.9
  93.5 66.8 %all-to-all-start.1 = ((bf16[8,24,7168]{2,1,0:T(8,128)(2,1)}), bf16[8,24,7168]{2,1,0:T(8,128)(2,1)S(1)}, u32[]{:S(2)}, u32[]{:S(2)}) async-start(bf16[8,24,7168]{2,1,0:T(8,128)(2,1)} %bitcast.234), calls=%async_computation.1 | async-start | bytes 5505024 | tf_op jit(solution)/shard_map/all_to_all | solution.py:86
  160.3 1.5 copy-start.4
  160.7 15.9 %copy-start.8 = (f32[1,7168]{1,0:T(1,128)S(1)}, f32[1,7168]{1,0:T(1,128)}, u32[]{:S(2)}) copy-start(f32[1,7168]{1,0:T(1,128)} %param.19) | copy-start | bytes 86020
  163.5 12.8 %collective-permute-start = (bf16[32,7168]{1,0:T(8,128)(2,1)S(1)}, bf16[32,7168]{1,0:T(8,128)(2,1)S(1)}, u32[]{:S(2)}, u32[]{:S(2)}) collective-permute-start(bf16[32,7168]{1,0:T(8,128)(2,1)S(1)} %get-tuple-element.553), channel_id=1, source_target_pairs={{0,8},{8,16},{16,24},{1,9},{9,17},{17,25},{2,10},{10,18},{18,26},{... | collective-permute-start | bytes 1376264 | tf_op jit(solution)/shard_map/ppermute | solution.py:25
  177.3 66.2 %copy-start = (bf16[1,7168,256]{2,1,0:T(8,128)(2,1)S(1)}, bf16[1,7168,256]{2,1,0:T(8,128)(2,1)}, u32[]{:S(2)}) copy-start(bf16[1,7168,256]{2,1,0:T(8,128)(2,1)} %param.20) | copy-start | bytes 11010052
  252.3 66.6 %all-to-all-start.3 = ((bf16[8,24,7168]{2,1,0:T(8,128)(2,1)}), bf16[8,24,7168]{2,1,0:T(8,128)(2,1)S(1)}, u32[]{:S(2)}, u32[]{:S(2)}) async-start(bf16[8,24,7168]{2,1,0:T(8,128)(2,1)} %bitcast.238), calls=%async_computation.3 | async-start | bytes 5505024 | tf_op jit(solution)/shard_map/all_to_all | solution.py:86
  318.9 17.1 %copy-start.5 = (bf16[2,32,7168]{2,1,0:T(8,128)(2,1)S(1)}, bf16[2,32,7168]{2,1,0:T(8,128)(2,1)}, u32[]{:S(2)}) copy-start(bf16[2,32,7168]{2,1,0:T(8,128)(2,1)} %param.18) | copy-start | bytes 2752516
  322.1 13.9 %collective-permute-start.1 = (bf16[32,7168]{1,0:T(8,128)(2,1)S(1)}, bf16[32,7168]{1,0:T(8,128)(2,1)S(1)}, u32[]{:S(2)}, u32[]{:S(2)}) collective-permute-start(bf16[32,7168]{1,0:T(8,128)(2,1)S(1)} %get-tuple-element.555), channel_id=1, source_target_pairs={{0,8},{8,16},{16,24},{1,9},{9,17},{17,25},{2,10},{10,18},{18,26},{... | collective-permute-start | bytes 1376264 | tf_op jit(solution)/shard_map/ppermute | solution.py:25
  337.0 66.2 %copy-start.1 = (bf16[1,7168,256]{2,1,0:T(8,128)(2,1)S(1)}, bf16[1,7168,256]{2,1,0:T(8,128)(2,1)}, u32[]{:S(2)}) copy-start(bf16[1,7168,256]{2,1,0:T(8,128)(2,1)} %param.20) | copy-start | bytes 11010052
  412.0 66.6 %all-to-all-start.5 = ((bf16[8,24,7168]{2,1,0:T(8,128)(2,1)}), bf16[8,24,7168]{2,1,0:T(8,128)(2,1)S(1)}, u32[]{:S(2)}, u32[]{:S(2)}) async-start(bf16[8,24,7168]{2,1,0:T(8,128)(2,1)} %bitcast.239), calls=%async_computation.5 | async-start | bytes 5505024 | tf_op jit(solution)/shard_map/all_to_all | solution.py:86
  478.6 17.0 %copy-start.6 = (bf16[2,32,7168]{2,1,0:T(8,128)(2,1)S(1)}, bf16[2,32,7168]{2,1,0:T(8,128)(2,1)}, u32[]{:S(2)}) copy-start(bf16[2,32,7168]{2,1,0:T(8,128)(2,1)} %param.18) | copy-start | bytes 2752516
  481.8 13.8 %collective-permute-start.2 = (bf16[32,7168]{1,0:T(8,128)(2,1)S(1)}, bf16[32,7168]{1,0:T(8,128)(2,1)S(1)}, u32[]{:S(2)}, u32[]{:S(2)}) collective-permute-start(bf16[32,7168]{1,0:T(8,128)(2,1)S(1)} %get-tuple-element.557), channel_id=1, source_target_pairs={{0,8},{8,16},{16,24},{1,9},{9,17},{17,25},{2,10},{10,18},{18,26},{... | collective-permute-start | bytes 1376264 | tf_op jit(solution)/shard_map/ppermute | solution.py:25
  496.7 66.2 %copy-start.2 = (bf16[1,7168,256]{2,1,0:T(8,128)(2,1)S(1)}, bf16[1,7168,256]{2,1,0:T(8,128)(2,1)}, u32[]{:S(2)}) copy-start(bf16[1,7168,256]{2,1,0:T(8,128)(2,1)} %param.20) | copy-start | bytes 11010052
  571.6 66.6 %all-to-all-start.7 = ((bf16[8,24,7168]{2,1,0:T(8,128)(2,1)}), bf16[8,24,7168]{2,1,0:T(8,128)(2,1)S(1)}, u32[]{:S(2)}, u32[]{:S(2)}) async-start(bf16[8,24,7168]{2,1,0:T(8,128)(2,1)} %bitcast.237), calls=%async_computation.7 | async-start | bytes 5505024 | tf_op jit(solution)/shard_map/all_to_all | solution.py:86
  638.3 17.9 %copy-start.7 = (bf16[2,32,7168]{2,1,0:T(8,128)(2,1)S(1)}, bf16[2,32,7168]{2,1,0:T(8,128)(2,1)}, u32[]{:S(2)}) copy-start(bf16[2,32,7168]{2,1,0:T(8,128)(2,1)} %param.18) | copy-start | bytes 2752516
  641.4 14.7 %collective-permute-start.3 = (bf16[32,7168]{1,0:T(8,128)(2,1)S(1)}, bf16[32,7168]{1,0:T(8,128)(2,1)S(1)}, u32[]{:S(2)}, u32[]{:S(2)}) collective-permute-start(bf16[32,7168]{1,0:T(8,128)(2,1)S(1)} %get-tuple-element.559), channel_id=1, source_target_pairs={{0,8},{8,16},{16,24},{1,9},{9,17},{17,25},{2,10},{10,18},{18,26},{... | collective-permute-start | bytes 1376264 | tf_op jit(solution)/shard_map/ppermute | solution.py:25
  657.2 66.2 %copy-start.3 = (bf16[1,7168,256]{2,1,0:T(8,128)(2,1)S(1)}, bf16[1,7168,256]{2,1,0:T(8,128)(2,1)}, u32[]{:S(2)}) copy-start(bf16[1,7168,256]{2,1,0:T(8,128)(2,1)} %param.20) | copy-start | bytes 11010052
  732.1 66.6 %all-to-all-start.9 = ((bf16[8,24,7168]{2,1,0:T(8,128)(2,1)}), bf16[8,24,7168]{2,1,0:T(8,128)(2,1)S(1)}, u32[]{:S(2)}, u32[]{:S(2)}) async-start(bf16[8,24,7168]{2,1,0:T(8,128)(2,1)} %bitcast.236), calls=%async_computation.9 | async-start | bytes 5505024 | tf_op jit(solution)/shard_map/all_to_all | solution.py:86
  735.7 95.2 %reduce-scatter.2.cloned.1.call-start = ((), (), s32[]{:S(2)}) async-start(), calls=%async_computation.11 | async-start | bytes 1146880 | tf_op jit(solution)/shard_map/reduce_scatter | solution.py:132
Sparse Core Ops, SparseCore 0:
  802.1 28.8 reduce-scatter.1
where the time goes:
time: 839 us; the launch traced here: 838 us
  waiting for transfers between devices  379 us (45%)
  blocking collectives  325 us (39%)
  matrix products  61.6 us (7%)
  starting transfers between devices  42.3 us (5%)
  between operations  14.6 us (2%)
    all_to_all x5, waiting for transfers between devices, moe_layer(): lax.all_to_all(partials, 'expert', split_axis=0, concat_axis=0, tiled=True)  313 us
    all_to_all x4, blocking collectives, moe_layer(): lax.all_to_all(outgoing, 'expert', split_axis=0, concat_axis=0, tiled=True)  265 us
    unnamed x1, blocking collectives  60.4 us
    dot_general x5, matrix products, expert_rows(): jnp.dot(hidden, down_rows, preferred_element_type=jnp.float32)  38.9 us
    ppermute x4, waiting for transfers between devices, shifted(): return lax.ppermute(array, axis, pairs)  37.5 us
    reduce_scatter x1, waiting for transfers between devices, body(): lax.psum_scatter(results.astype(jnp.float32).astype(jnp.bfloat16), 'secti...  29 us
    all_to_all x5, starting transfers between devices, moe_layer(): lax.all_to_all(partials, 'expert', split_axis=0, concat_axis=0, tiled=True)  18.3 us
    ppermute x4, starting transfers between devices, shifted(): return lax.ppermute(array, axis, pairs)  17.4 us
  transfers between devices with their start and end apart: 11, of which 10 were waited for; matrix products, arithmetic and copies ran while one was open for 1% of the time, Pallas kernels for 0%

commit v1 on v0

--- a/solution.py
+++ b/solution.py
@@ -4,6 +4,29 @@
 from jax.sharding import PartitionSpec as P
 
 EPSILON = 1e-06
+
+
+def split_up(array, dim, size):
+    dims = array.shape
+    pieces = array.reshape(*dims[:dim], size, dims[dim] // size, *dims[dim + 1 :])
+    return jnp.moveaxis(pieces, dim, 0)
+
+
+def joined_along(pieces, dim):
+    pieces = jnp.moveaxis(pieces, 0, dim)
+    shape = pieces.shape
+    return pieces.reshape(*shape[:dim], shape[dim] * shape[dim + 1], *shape[dim + 2 :])
+
+
+def exchange_directly(x, axis, split_dim, concat_dim):
+    peers, index = (lax.axis_size(axis), lax.axis_index(axis))
+    blocks = split_up(x, split_dim, peers)
+    outs = [blocks[index]]
+    for step in range(1, peers):
+        sent = blocks[(index + step) % peers]
+        outs.append(lax.ppermute(sent, axis, [(i, (i + step) % peers) for i in range(peers)]))
+    blocks = jnp.stack(outs)[(index - jnp.arange(peers)) % peers]
+    return joined_along(blocks, concat_dim)
 
 
 def entering(array, axis, combine, identity):
@@ -78,10 +101,7 @@
     ).astype(jnp.bfloat16)
     outgoing = jnp.repeat(packed.reshape(expert_total, slot_count, width), split_count, axis=0)
     partials = expert_rows(
-        lax.all_to_all(outgoing, "expert", split_axis=0, concat_axis=0, tiled=True),
-        gate_cols,
-        up_cols,
-        down_rows,
+        exchange_directly(outgoing, "expert", 0, 0), gate_cols, up_cols, down_rows
     )
     returned = lax.all_to_all(partials, "expert", split_axis=0, concat_axis=0, tiled=True)
     summed = jnp.sum(

time: 839 us -> 857 us (1.021)
  blocking collectives: 325 us -> 39.7 us
  waiting for transfers between devices: 379 us -> 518 us
  starting transfers between devices: 42.3 us -> 165 us
  local copies, waits for them, and re-layouts: 7 us -> 31.8 us
    all_to_all x4 -> x0, blocking collectives: 265 us -> none  [moe_layer(): lax.all_to_all(outgoing, 'expert', split_axis=0, concat_axis=0, tiled=True)]
    ppermute x0 -> x35, waiting for transfers between devices: none -> 139 us  [exchange_directly(): lax.ppermute(sent, axis, [(i, (i + step) % peers) for i in range(peers)])]
    all_to_all x5, starting transfers between devices: 18.3 us -> 89.8 us  [moe_layer(): lax.all_to_all(partials, 'expert', split_axis=0, concat_axis=0, tiled=True)]
    ppermute x0 -> x35, starting transfers between devices: none -> 57.8 us  [exchange_directly(): lax.ppermute(sent, axis, [(i, (i + step) % peers) for i in range(peers)])]
    unnamed x1, blocking collectives: 60.4 us -> 39.7 us
    gather x0 -> x5, local copies, waits for them, and re-layouts: none -> 12.5 us  [exchange_directly(): blocks = jnp.stack(outs)[(index - jnp.arange(peers)) % peers]]
    unnamed x35 -> x67, local copies, waits for them, and re-layouts: 1.77 us -> 13.1 us
  transfers between devices with their start and end apart: 11 -> 45, of which waited for: 10 -> 32; matrix products, arithmetic and copies ran while one was open for 1% -> 1% of each run, Pallas kernels for 0% -> 0%
where the time goes in v1:
time: 857 us; the launch traced here: 848 us
  waiting for transfers between devices  518 us (60%)
  starting transfers between devices  165 us (19%)
  matrix products  69.6 us (8%)
  blocking collectives  39.7 us (5%)
  local copies, waits for them, and re-layouts  31.8 us (4%)
  between operations  15.3 us (2%)
    all_to_all x5, waiting for transfers between devices, moe_layer(): lax.all_to_all(partials, 'expert', split_axis=0, concat_axis=0, tiled=True)  313 us
    ppermute x35, waiting for transfers between devices, exchange_directly(): lax.ppermute(sent, axis, [(i, (i + step) % peers) for i in range(peers)])  139 us
    all_to_all x5, starting transfers between devices, moe_layer(): lax.all_to_all(partials, 'expert', split_axis=0, concat_axis=0, tiled=True)  89.8 us
    ppermute x35, starting transfers between devices, exchange_directly(): lax.ppermute(sent, axis, [(i, (i + step) % peers) for i in range(peers)])  57.8 us
    unnamed x1, blocking collectives  39.7 us
    dot_general x5, matrix products, expert_rows(): jnp.dot(hidden, down_rows, preferred_element_type=jnp.float32)  38.9 us
    ppermute x4, waiting for transfers between devices, shifted(): return lax.ppermute(array, axis, pairs)  37.5 us
    reduce_scatter x1, waiting for transfers between devices, body(): lax.psum_scatter(results.astype(jnp.float32).astype(jnp.bfloat16), 'secti...  29 us
  transfers between devices with their start and end apart: 45, of which 32 were waited for; matrix products, arithmetic and copies ran while one was open for 1% of the time, Pallas kernels for 0%

profile of v1, /device:TPU:0, one launch (start us, length us, event | category | flops | bytes accessed | tf_op | source)
XLA Modules:
  0.0 847.6 jit_solution(10725967930479506055)
XLA Ops:
  22.9 39.7 %all-reduce.5 = (s32[16]{0:T(128)S(1)}, s32[16]{0:T(128)S(1)}, s32[16]{0:T(128)S(1)}, s32[16]{0:T(128)S(1)}, s32[16]{0:T(128)S(1)}) all-reduce(s32[16]{0:T(128)S(1)} %dynamic-update-slice.9, s32[16]{0:T(128)S(1)} %dynamic-update-slice.6, s32[16]{0:T(128)S(1)} %dynamic-update-slice.7, ...), channel_id=6, replica_groups=mesh['section'=4,'expert'=8] {'expert'}, use_global_device_ids=true, to_apply=%add.4 | all-reduce | flops 80 | bytes 640
  87.1 7.8 convolution_convert_fusion.4
  101.5 61.5 %all-to-all-done = bf16[8,24,7168]{2,1,0:T(8,128)(2,1)S(1)} async-done(((bf16[8,24,7168]{2,1,0:T(8,128)(2,1)}), bf16[8,24,7168]{2,1,0:T(8,128)(2,1)S(1)}, u32[]{:S(2)}, u32[]{:S(2)}) %all-to-all-start) | async-done | bytes 2752544 | tf_op jit(solution)/shard_map/all_to_all | solution.py:106
  169.6 9.4 %collective-permute-done.7 = bf16[32,7168]{1,0:T(8,128)(2,1)S(1)} collective-permute-done((bf16[32,7168]{1,0:T(8,128)(2,1)S(1)}, bf16[32,7168]{1,0:T(8,128)(2,1)S(1)}, u32[]{:S(2)}, u32[]{:S(2)}) %collective-permute-start.7) | collective-permute-done | bytes 458784 | tf_op jit(solution)/shard_map/ppermute | solution.py:48
  185.1 6.9 collective-permute-done.8
  193.3 6.3 collective-permute-start.14
  199.6 22.3 %collective-permute-done.10 = bf16[1,24,7168]{2,1,0:T(8,128)(2,1)S(1)} collective-permute-done((bf16[1,24,7168]{2,1,0:T(8,128)(2,1)S(1)}, bf16[1,24,7168]{2,1,0:T(8,128)(2,1)S(1)}, u32[]{:S(2)}, u32[]{:S(2)}) %collective-permute-start.10) | collective-permute-done | bytes 344096 | tf_op jit(solution)/shard_map/ppermute | solution.py:27
  231.2 7.8 convolution_convert_fusion.3
  239.0 21.2 %all-to-all-start.1 = ((bf16[8,24,7168]{2,1,0:T(8,128)(2,1)}), bf16[8,24,7168]{2,1,0:T(8,128)(2,1)S(1)}, u32[]{:S(2)}, u32[]{:S(2)}) async-start(bf16[8,24,7168]{2,1,0:T(8,128)(2,1)} %bitcast.384), calls=%async_computation.1 | async-start | bytes 5505024 | tf_op jit(solution)/shard_map/all_to_all | solution.py:106
  260.3 62.9 %all-to-all-done.1 = bf16[8,24,7168]{2,1,0:T(8,128)(2,1)S(1)} async-done(((bf16[8,24,7168]{2,1,0:T(8,128)(2,1)}), bf16[8,24,7168]{2,1,0:T(8,128)(2,1)S(1)}, u32[]{:S(2)}, u32[]{:S(2)}) %all-to-all-start.1) | async-done | bytes 2752544 | tf_op jit(solution)/shard_map/all_to_all | solution.py:106
  330.9 9.4 %collective-permute-done.15 = bf16[32,7168]{1,0:T(8,128)(2,1)S(1)} collective-permute-done((bf16[32,7168]{1,0:T(8,128)(2,1)S(1)}, bf16[32,7168]{1,0:T(8,128)(2,1)S(1)}, u32[]{:S(2)}, u32[]{:S(2)}) %collective-permute-start.15) | collective-permute-done | bytes 458784 | tf_op jit(solution)/shard_map/ppermute | solution.py:48
  346.5 6.8 collective-permute-done.16
  354.7 6.0 collective-permute-start.22
  360.7 22.6 %collective-permute-done.18 = bf16[1,24,7168]{2,1,0:T(8,128)(2,1)S(1)} collective-permute-done((bf16[1,24,7168]{2,1,0:T(8,128)(2,1)S(1)}, bf16[1,24,7168]{2,1,0:T(8,128)(2,1)S(1)}, u32[]{:S(2)}, u32[]{:S(2)}) %collective-permute-start.18) | collective-permute-done | bytes 344096 | tf_op jit(solution)/shard_map/ppermute | solution.py:27
  392.6 7.8 convolution_convert_fusion.2
  400.4 21.3 %all-to-all-start.2 = ((bf16[8,24,7168]{2,1,0:T(8,128)(2,1)}), bf16[8,24,7168]{2,1,0:T(8,128)(2,1)S(1)}, u32[]{:S(2)}, u32[]{:S(2)}) async-start(bf16[8,24,7168]{2,1,0:T(8,128)(2,1)} %bitcast.385), calls=%async_computation.2 | async-start | bytes 5505024 | tf_op jit(solution)/shard_map/all_to_all | solution.py:106
  421.9 62.9 %all-to-all-done.2 = bf16[8,24,7168]{2,1,0:T(8,128)(2,1)S(1)} async-done(((bf16[8,24,7168]{2,1,0:T(8,128)(2,1)}), bf16[8,24,7168]{2,1,0:T(8,128)(2,1)S(1)}, u32[]{:S(2)}, u32[]{:S(2)}) %all-to-all-start.2) | async-done | bytes 2752544 | tf_op jit(solution)/shard_map/all_to_all | solution.py:106
  492.6 9.3 %collective-permute-done.23 = bf16[32,7168]{1,0:T(8,128)(2,1)S(1)} collective-permute-done((bf16[32,7168]{1,0:T(8,128)(2,1)S(1)}, bf16[32,7168]{1,0:T(8,128)(2,1)S(1)}, u32[]{:S(2)}, u32[]{:S(2)}) %collective-permute-start.23) | collective-permute-done | bytes 458784 | tf_op jit(solution)/shard_map/ppermute | solution.py:48
  508.0 6.9 collective-permute-done.24
  516.2 6.0 collective-permute-start.30
  522.2 22.6 %collective-permute-done.26 = bf16[1,24,7168]{2,1,0:T(8,128)(2,1)S(1)} collective-permute-done((bf16[1,24,7168]{2,1,0:T(8,128)(2,1)S(1)}, bf16[1,24,7168]{2,1,0:T(8,128)(2,1)S(1)}, u32[]{:S(2)}, u32[]{:S(2)}) %collective-permute-start.26) | collective-permute-done | bytes 344096 | tf_op jit(solution)/shard_map/ppermute | solution.py:27
  554.1 7.8 convolution_convert_fusion.1
  561.9 21.1 %all-to-all-start.3 = ((bf16[8,24,7168]{2,1,0:T(8,128)(2,1)}), bf16[8,24,7168]{2,1,0:T(8,128)(2,1)S(1)}, u32[]{:S(2)}, u32[]{:S(2)}) async-start(bf16[8,24,7168]{2,1,0:T(8,128)(2,1)} %bitcast.383), calls=%async_computation.3 | async-start | bytes 5505024 | tf_op jit(solution)/shard_map/all_to_all | solution.py:106
  583.2 62.9 %all-to-all-done.3 = bf16[8,24,7168]{2,1,0:T(8,128)(2,1)S(1)} async-done(((bf16[8,24,7168]{2,1,0:T(8,128)(2,1)}), bf16[8,24,7168]{2,1,0:T(8,128)(2,1)S(1)}, u32[]{:S(2)}, u32[]{:S(2)}) %all-to-all-start.3) | async-done | bytes 2752544 | tf_op jit(solution)/shard_map/all_to_all | solution.py:106
  654.6 9.4 %collective-permute-done.31 = bf16[32,7168]{1,0:T(8,128)(2,1)S(1)} collective-permute-done((bf16[32,7168]{1,0:T(8,128)(2,1)S(1)}, bf16[32,7168]{1,0:T(8,128)(2,1)S(1)}, u32[]{:S(2)}, u32[]{:S(2)}) %collective-permute-start.31) | collective-permute-done | bytes 458784 | tf_op jit(solution)/shard_map/ppermute | solution.py:48
  670.2 6.9 collective-permute-done.32
  678.3 6.2 collective-permute-start.38
  684.5 22.4 %collective-permute-done.34 = bf16[1,24,7168]{2,1,0:T(8,128)(2,1)S(1)} collective-permute-done((bf16[1,24,7168]{2,1,0:T(8,128)(2,1)S(1)}, bf16[1,24,7168]{2,1,0:T(8,128)(2,1)S(1)}, u32[]{:S(2)}, u32[]{:S(2)}) %collective-permute-start.34) | collective-permute-done | bytes 344096 | tf_op jit(solution)/shard_map/ppermute | solution.py:27
  716.3 7.8 convolution_convert_fusion
  724.1 21.1 %all-to-all-start.4 = ((bf16[8,24,7168]{2,1,0:T(8,128)(2,1)}), bf16[8,24,7168]{2,1,0:T(8,128)(2,1)S(1)}, u32[]{:S(2)}, u32[]{:S(2)}) async-start(bf16[8,24,7168]{2,1,0:T(8,128)(2,1)} %bitcast.382), calls=%async_computation.4 | async-start | bytes 5505024 | tf_op jit(solution)/shard_map/all_to_all | solution.py:106
  745.4 62.9 %all-to-all-done.4 = bf16[8,24,7168]{2,1,0:T(8,128)(2,1)S(1)} async-done(((bf16[8,24,7168]{2,1,0:T(8,128)(2,1)}), bf16[8,24,7168]{2,1,0:T(8,128)(2,1)S(1)}, u32[]{:S(2)}, u32[]{:S(2)}) %all-to-all-start.4) | async-done | bytes 2752544 | tf_op jit(solution)/shard_map/all_to_all | solution.py:106
  811.5 29.0 %reduce-scatter.2.cloned.1.call-done = bf16[2,32,1792]{2,1,0:T(8,128)(2,1)} async-done(((bf16[2,32,7168]{2,1,0:T(8,128)(2,1)}), bf16[2,32,1792]{2,1,0:T(8,128)(2,1)}) %reduce-scatter.2.cloned.1.call-update) | async-done | bytes 229392 | tf_op jit(solution)/shard_map/reduce_scatter | solution.py:152
  (260 shorter events, 148.1 us)
Async XLA Ops:
  12.1 51.4 %collective-permute-start = (bf16[1,24,7168]{2,1,0:T(8,128)(2,1)}, bf16[1,24,7168]{2,1,0:T(8,128)(2,1)}, u32[]{:S(2)}, u32[]{:S(2)}) collective-permute-start(bf16[1,24,7168]{2,1,0:T(8,128)(2,1)} %get-tuple-element.581), channel_id=1, source_target_pairs={{0,1},{1,2},{2,3},{3,4},{4,5},{5,6},{6,7},{7,0},{8,9},{9,10},{10,1... | collective-permute-start | bytes 1032200 | tf_op jit(solution)/shard_map/ppermute | solution.py:27
  12.6 57.7 %collective-permute-start.1 = (bf16[1,24,7168]{2,1,0:T(8,128)(2,1)}, bf16[1,24,7168]{2,1,0:T(8,128)(2,1)}, u32[]{:S(2)}, u32[]{:S(2)}) collective-permute-start(bf16[1,24,7168]{2,1,0:T(8,128)(2,1)} %get-tuple-element.580), channel_id=1, source_target_pairs={{0,2},{1,3},{2,4},{3,5},{4,6},{5,7},{6,0},{7,1},{8,10},{9,11},{10,... | collective-permute-start | bytes 1032200 | tf_op jit(solution)/shard_map/ppermute | solution.py:27
  15.2 56.3 %collective-permute-start.2 = (bf16[1,24,7168]{2,1,0:T(8,128)(2,1)}, bf16[1,24,7168]{2,1,0:T(8,128)(2,1)}, u32[]{:S(2)}, u32[]{:S(2)}) collective-permute-start(bf16[1,24,7168]{2,1,0:T(8,128)(2,1)} %get-tuple-element.579), channel_id=1, source_target_pairs={{0,3},{1,4},{2,5},{3,6},{4,7},{5,0},{6,1},{7,2},{8,11},{9,12},{10,... | collective-permute-start | bytes 1032200 | tf_op jit(solution)/shard_map/ppermute | solution.py:27
  17.8 54.7 %collective-permute-start.3 = (bf16[1,24,7168]{2,1,0:T(8,128)(2,1)}, bf16[1,24,7168]{2,1,0:T(8,128)(2,1)S(1)}, u32[]{:S(2)}, u32[]{:S(2)}) collective-permute-start(bf16[1,24,7168]{2,1,0:T(8,128)(2,1)} %get-tuple-element.578), channel_id=1, source_target_pairs={{0,4},{1,5},{2,6},{3,7},{4,0},{5,1},{6,2},{7,3},{8,12},{9,13},{10,... | collective-permute-start | bytes 1032200 | tf_op jit(solution)/shard_map/ppermute | solution.py:27
  19.0 53.5 %collective-permute-start.4 = (bf16[1,24,7168]{2,1,0:T(8,128)(2,1)}, bf16[1,24,7168]{2,1,0:T(8,128)(2,1)S(1)}, u32[]{:S(2)}, u32[]{:S(2)}) collective-permute-start(bf16[1,24,7168]{2,1,0:T(8,128)(2,1)} %get-tuple-element.577), channel_id=1, source_target_pairs={{0,5},{1,6},{2,7},{3,0},{4,1},{5,2},{6,3},{7,4},{8,13},{9,14},{10,... | collective-permute-start | bytes 1032200 | tf_op jit(solution)/shard_map/ppermute | solution.py:27
  94.9 68.1 %all-to-all-start = ((bf16[8,24,7168]{2,1,0:T(8,128)(2,1)}), bf16[8,24,7168]{2,1,0:T(8,128)(2,1)S(1)}, u32[]{:S(2)}, u32[]{:S(2)}) async-start(bf16[8,24,7168]{2,1,0:T(8,128)(2,1)} %bitcast.381), calls=%async_computation | async-start | bytes 5505024 | tf_op jit(solution)/shard_map/all_to_all | solution.py:106
  180.4 41.5 %collective-permute-start.10 = (bf16[1,24,7168]{2,1,0:T(8,128)(2,1)S(1)}, bf16[1,24,7168]{2,1,0:T(8,128)(2,1)S(1)}, u32[]{:S(2)}, u32[]{:S(2)}) collective-permute-start(bf16[1,24,7168]{2,1,0:T(8,128)(2,1)S(1)} %get-tuple-element.571), channel_id=1, source_target_pairs={{0,3},{1,4},{2,5},{3,6},{4,7},{5,0},{6,1},{7,2},{8,11},{9,12},{10,... | collective-permute-start | bytes 1032200 | tf_op jit(solution)/shard_map/ppermute | solution.py:27
  182.7 39.4 %collective-permute-start.11 = (bf16[1,24,7168]{2,1,0:T(8,128)(2,1)S(1)}, bf16[1,24,7168]{2,1,0:T(8,128)(2,1)S(1)}, u32[]{:S(2)}, u32[]{:S(2)}) collective-permute-start(bf16[1,24,7168]{2,1,0:T(8,128)(2,1)S(1)} %get-tuple-element.570), channel_id=1, source_target_pairs={{0,4},{1,5},{2,6},{3,7},{4,0},{5,1},{6,2},{7,3},{8,12},{9,13},{10,... | collective-permute-start | bytes 1032200 | tf_op jit(solution)/shard_map/ppermute | solution.py:27
  184.4 37.7 %collective-permute-start.12 = (bf16[1,24,7168]{2,1,0:T(8,128)(2,1)S(1)}, bf16[1,24,7168]{2,1,0:T(8,128)(2,1)S(1)}, u32[]{:S(2)}, u32[]{:S(2)}) collective-permute-start(bf16[1,24,7168]{2,1,0:T(8,128)(2,1)S(1)} %get-tuple-element.569), channel_id=1, source_target_pairs={{0,5},{1,6},{2,7},{3,0},{4,1},{5,2},{6,3},{7,4},{8,13},{9,14},{10,... | collective-permute-start | bytes 1032200 | tf_op jit(solution)/shard_map/ppermute | solution.py:27
  192.0 30.1 %collective-permute-start.13 = (bf16[1,24,7168]{2,1,0:T(8,128)(2,1)S(1)}, bf16[1,24,7168]{2,1,0:T(8,128)(2,1)S(1)}, u32[]{:S(2)}, u32[]{:S(2)}) collective-permute-start(bf16[1,24,7168]{2,1,0:T(8,128)(2,1)S(1)} %get-tuple-element.568), channel_id=1, source_target_pairs={{0,6},{1,7},{2,0},{3,1},{4,2},{5,3},{6,4},{7,5},{8,14},{9,15},{10,... | collective-permute-start | bytes 1032200 | tf_op jit(solution)/shard_map/ppermute | solution.py:27
  193.3 30.9 %collective-permute-start.14 = (bf16[1,24,7168]{2,1,0:T(8,128)(2,1)S(1)}, bf16[1,24,7168]{2,1,0:T(8,128)(2,1)S(1)}, u32[]{:S(2)}, u32[]{:S(2)}) collective-permute-start(bf16[1,24,7168]{2,1,0:T(8,128)(2,1)S(1)} %get-tuple-element.567), channel_id=1, source_target_pairs={{0,7},{1,0},{2,1},{3,2},{4,3},{5,4},{6,5},{7,6},{8,15},{9,8},{10,9... | collective-permute-start | bytes 1032200 | tf_op jit(solution)/shard_map/ppermute | solution.py:27
  239.0 84.3 %all-to-all-start.1 = ((bf16[8,24,7168]{2,1,0:T(8,128)(2,1)}), bf16[8,24,7168]{2,1,0:T(8,128)(2,1)S(1)}, u32[]{:S(2)}, u32[]{:S(2)}) async-start(bf16[8,24,7168]{2,1,0:T(8,128)(2,1)} %bitcast.384), calls=%async_computation.1 | async-start | bytes 5505024 | tf_op jit(solution)/shard_map/all_to_all | solution.py:106
  341.8 41.5 %collective-permute-start.18 = (bf16[1,24,7168]{2,1,0:T(8,128)(2,1)S(1)}, bf16[1,24,7168]{2,1,0:T(8,128)(2,1)S(1)}, u32[]{:S(2)}, u32[]{:S(2)}) collective-permute-start(bf16[1,24,7168]{2,1,0:T(8,128)(2,1)S(1)} %get-tuple-element.563), channel_id=1, source_target_pairs={{0,3},{1,4},{2,5},{3,6},{4,7},{5,0},{6,1},{7,2},{8,11},{9,12},{10,... | collective-permute-start | bytes 1032200 | tf_op jit(solution)/shard_map/ppermute | solution.py:27
  344.1 39.4 %collective-permute-start.19 = (bf16[1,24,7168]{2,1,0:T(8,128)(2,1)S(1)}, bf16[1,24,7168]{2,1,0:T(8,128)(2,1)S(1)}, u32[]{:S(2)}, u32[]{:S(2)}) collective-permute-start(bf16[1,24,7168]{2,1,0:T(8,128)(2,1)S(1)} %get-tuple-element.562), channel_id=1, source_target_pairs={{0,4},{1,5},{2,6},{3,7},{4,0},{5,1},{6,2},{7,3},{8,12},{9,13},{10,... | collective-permute-start | bytes 1032200 | tf_op jit(solution)/shard_map/ppermute | solution.py:27
  345.8 37.7 %collective-permute-start.20 = (bf16[1,24,7168]{2,1,0:T(8,128)(2,1)S(1)}, bf16[1,24,7168]{2,1,0:T(8,128)(2,1)S(1)}, u32[]{:S(2)}, u32[]{:S(2)}) collective-permute-start(bf16[1,24,7168]{2,1,0:T(8,128)(2,1)S(1)} %get-tuple-element.561), channel_id=1, source_target_pairs={{0,5},{1,6},{2,7},{3,0},{4,1},{5,2},{6,3},{7,4},{8,13},{9,14},{10,... | collective-permute-start | bytes 1032200 | tf_op jit(solution)/shard_map/ppermute | solution.py:27
  353.4 30.1 %collective-permute-start.21 = (bf16[1,24,7168]{2,1,0:T(8,128)(2,1)S(1)}, bf16[1,24,7168]{2,1,0:T(8,128)(2,1)S(1)}, u32[]{:S(2)}, u32[]{:S(2)}) collective-permute-start(bf16[1,24,7168]{2,1,0:T(8,128)(2,1)S(1)} %get-tuple-element.560), channel_id=1, source_target_pairs={{0,6},{1,7},{2,0},{3,1},{4,2},{5,3},{6,4},{7,5},{8,14},{9,15},{10,... | collective-permute-start | bytes 1032200 | tf_op jit(solution)/shard_map/ppermute | solution.py:27
  354.7 31.0 %collective-permute-start.22 = (bf16[1,24,7168]{2,1,0:T(8,128)(2,1)S(1)}, bf16[1,24,7168]{2,1,0:T(8,128)(2,1)S(1)}, u32[]{:S(2)}, u32[]{:S(2)}) collective-permute-start(bf16[1,24,7168]{2,1,0:T(8,128)(2,1)S(1)} %get-tuple-element.559), channel_id=1, source_target_pairs={{0,7},{1,0},{2,1},{3,2},{4,3},{5,4},{6,5},{7,6},{8,15},{9,8},{10,9... | collective-permute-start | bytes 1032200 | tf_op jit(solution)/shard_map/ppermute | solution.py:27
  400.4 84.4 %all-to-all-start.2 = ((bf16[8,24,7168]{2,1,0:T(8,128)(2,1)}), bf16[8,24,7168]{2,1,0:T(8,128)(2,1)S(1)}, u32[]{:S(2)}, u32[]{:S(2)}) async-start(bf16[8,24,7168]{2,1,0:T(8,128)(2,1)} %bitcast.385), calls=%async_computation.2 | async-start | bytes 5505024 | tf_op jit(solution)/shard_map/all_to_all | solution.py:106
  503.2 41.5 %collective-permute-start.26 = (bf16[1,24,7168]{2,1,0:T(8,128)(2,1)S(1)}, bf16[1,24,7168]{2,1,0:T(8,128)(2,1)S(1)}, u32[]{:S(2)}, u32[]{:S(2)}) collective-permute-start(bf16[1,24,7168]{2,1,0:T(8,128)(2,1)S(1)} %get-tuple-element.555), channel_id=1, source_target_pairs={{0,3},{1,4},{2,5},{3,6},{4,7},{5,0},{6,1},{7,2},{8,11},{9,12},{10,... | collective-permute-start | bytes 1032200 | tf_op jit(solution)/shard_map/ppermute | solution.py:27
  505.6 39.4 %collective-permute-start.27 = (bf16[1,24,7168]{2,1,0:T(8,128)(2,1)S(1)}, bf16[1,24,7168]{2,1,0:T(8,128)(2,1)S(1)}, u32[]{:S(2)}, u32[]{:S(2)}) collective-permute-start(bf16[1,24,7168]{2,1,0:T(8,128)(2,1)S(1)} %get-tuple-element.554), channel_id=1, source_target_pairs={{0,4},{1,5},{2,6},{3,7},{4,0},{5,1},{6,2},{7,3},{8,12},{9,13},{10,... | collective-permute-start | bytes 1032200 | tf_op jit(solution)/shard_map/ppermute | solution.py:27
  507.3 37.7 %collective-permute-start.28 = (bf16[1,24,7168]{2,1,0:T(8,128)(2,1)S(1)}, bf16[1,24,7168]{2,1,0:T(8,128)(2,1)S(1)}, u32[]{:S(2)}, u32[]{:S(2)}) collective-permute-start(bf16[1,24,7168]{2,1,0:T(8,128)(2,1)S(1)} %get-tuple-element.553), channel_id=1, source_target_pairs={{0,5},{1,6},{2,7},{3,0},{4,1},{5,2},{6,3},{7,4},{8,13},{9,14},{10,... | collective-permute-start | bytes 1032200 | tf_op jit(solution)/shard_map/ppermute | solution.py:27
  514.9 30.1 %collective-permute-start.29 = (bf16[1,24,7168]{2,1,0:T(8,128)(2,1)S(1)}, bf16[1,24,7168]{2,1,0:T(8,128)(2,1)S(1)}, u32[]{:S(2)}, u32[]{:S(2)}) collective-permute-start(bf16[1,24,7168]{2,1,0:T(8,128)(2,1)S(1)} %get-tuple-element.552), channel_id=1, source_target_pairs={{0,6},{1,7},{2,0},{3,1},{4,2},{5,3},{6,4},{7,5},{8,14},{9,15},{10,... | collective-permute-start | bytes 1032200 | tf_op jit(solution)/shard_map/ppermute | solution.py:27
  516.2 30.9 %collective-permute-start.30 = (bf16[1,24,7168]{2,1,0:T(8,128)(2,1)S(1)}, bf16[1,24,7168]{2,1,0:T(8,128)(2,1)S(1)}, u32[]{:S(2)}, u32[]{:S(2)}) collective-permute-start(bf16[1,24,7168]{2,1,0:T(8,128)(2,1)S(1)} %get-tuple-element.551), channel_id=1, source_target_pairs={{0,7},{1,0},{2,1},{3,2},{4,3},{5,4},{6,5},{7,6},{8,15},{9,8},{10,9... | collective-permute-start | bytes 1032200 | tf_op jit(solution)/shard_map/ppermute | solution.py:27
  561.9 84.2 %all-to-all-start.3 = ((bf16[8,24,7168]{2,1,0:T(8,128)(2,1)}), bf16[8,24,7168]{2,1,0:T(8,128)(2,1)S(1)}, u32[]{:S(2)}, u32[]{:S(2)}) async-start(bf16[8,24,7168]{2,1,0:T(8,128)(2,1)} %bitcast.383), calls=%async_computation.3 | async-start | bytes 5505024 | tf_op jit(solution)/shard_map/all_to_all | solution.py:106
  649.3 14.7 %collective-permute-start.31 = (bf16[32,7168]{1,0:T(8,128)(2,1)S(1)}, bf16[32,7168]{1,0:T(8,128)(2,1)S(1)}, u32[]{:S(2)}, u32[]{:S(2)}) collective-permute-start(bf16[32,7168]{1,0:T(8,128)(2,1)S(1)} %get-tuple-element.599), channel_id=1, source_target_pairs={{0,8},{8,16},{16,24},{1,9},{9,17},{17,25},{2,10},{10,18},{18,26},{... | collective-permute-start | bytes 1376264 | tf_op jit(solution)/shard_map/ppermute | solution.py:48
  665.4 41.5 %collective-permute-start.34 = (bf16[1,24,7168]{2,1,0:T(8,128)(2,1)S(1)}, bf16[1,24,7168]{2,1,0:T(8,128)(2,1)S(1)}, u32[]{:S(2)}, u32[]{:S(2)}) collective-permute-start(bf16[1,24,7168]{2,1,0:T(8,128)(2,1)S(1)} %get-tuple-element.547), channel_id=1, source_target_pairs={{0,3},{1,4},{2,5},{3,6},{4,7},{5,0},{6,1},{7,2},{8,11},{9,12},{10,... | collective-permute-start | bytes 1032200 | tf_op jit(solution)/shard_map/ppermute | solution.py:27
  667.8 39.4 %collective-permute-start.35 = (bf16[1,24,7168]{2,1,0:T(8,128)(2,1)S(1)}, bf16[1,24,7168]{2,1,0:T(8,128)(2,1)S(1)}, u32[]{:S(2)}, u32[]{:S(2)}) collective-permute-start(bf16[1,24,7168]{2,1,0:T(8,128)(2,1)S(1)} %get-tuple-element.546), channel_id=1, source_target_pairs={{0,4},{1,5},{2,6},{3,7},{4,0},{5,1},{6,2},{7,3},{8,12},{9,13},{10,... | collective-permute-start | bytes 1032200 | tf_op jit(solution)/shard_map/ppermute | solution.py:27
  669.4 37.7 %collective-permute-start.36 = (bf16[1,24,7168]{2,1,0:T(8,128)(2,1)S(1)}, bf16[1,24,7168]{2,1,0:T(8,128)(2,1)S(1)}, u32[]{:S(2)}, u32[]{:S(2)}) collective-permute-start(bf16[1,24,7168]{2,1,0:T(8,128)(2,1)S(1)} %get-tuple-element.545), channel_id=1, source_target_pairs={{0,5},{1,6},{2,7},{3,0},{4,1},{5,2},{6,3},{7,4},{8,13},{9,14},{10,... | collective-permute-start | bytes 1032200 | tf_op jit(solution)/shard_map/ppermute | solution.py:27
  677.0 30.1 %collective-permute-start.37 = (bf16[1,24,7168]{2,1,0:T(8,128)(2,1)S(1)}, bf16[1,24,7168]{2,1,0:T(8,128)(2,1)S(1)}, u32[]{:S(2)}, u32[]{:S(2)}) collective-permute-start(bf16[1,24,7168]{2,1,0:T(8,128)(2,1)S(1)} %get-tuple-element.544), channel_id=1, source_target_pairs={{0,6},{1,7},{2,0},{3,1},{4,2},{5,3},{6,4},{7,5},{8,14},{9,15},{10,... | collective-permute-start | bytes 1032200 | tf_op jit(solution)/shard_map/ppermute | solution.py:27
  678.3 31.0 %collective-permute-start.38 = (bf16[1,24,7168]{2,1,0:T(8,128)(2,1)S(1)}, bf16[1,24,7168]{2,1,0:T(8,128)(2,1)S(1)}, u32[]{:S(2)}, u32[]{:S(2)}) collective-permute-start(bf16[1,24,7168]{2,1,0:T(8,128)(2,1)S(1)} %get-tuple-element.543), channel_id=1, source_target_pairs={{0,7},{1,0},{2,1},{3,2},{4,3},{5,4},{6,5},{7,6},{8,15},{9,8},{10,9... | collective-permute-start | bytes 1032200 | tf_op jit(solution)/shard_map/ppermute | solution.py:27
  724.1 84.2 %all-to-all-start.4 = ((bf16[8,24,7168]{2,1,0:T(8,128)(2,1)}), bf16[8,24,7168]{2,1,0:T(8,128)(2,1)S(1)}, u32[]{:S(2)}, u32[]{:S(2)}) async-start(bf16[8,24,7168]{2,1,0:T(8,128)(2,1)} %bitcast.382), calls=%async_computation.4 | async-start | bytes 5505024 | tf_op jit(solution)/shard_map/all_to_all | solution.py:106
  745.2 95.3 %reduce-scatter.2.cloned.1.call-start = ((), (), s32[]{:S(2)}) async-start(), calls=%async_computation.6 | async-start | bytes 1146880 | tf_op jit(solution)/shard_map/reduce_scatter | solution.py:152
  (26 other events, 261.7 us)
Sparse Core Ops, SparseCore 0:
  811.6 28.8 reduce-scatter.1
